TPU v7x, 32 devices: a whole 2x2x4 slice. The times are simulated.
32 devices in a mesh: set: 4 (over z), path: 2 (over y), tm: 4 (over x, core).
Axes of the slice: x: 2, y: 2, z: 4, core: 2. Of those that a mesh axis runs over, the one named last changes fastest.
Arguments:
- normals: bfloat16 [1024, 2048], P(('set', 'path'), 'tm'), parts along dimension 0, may hold values from -6 to 6
- orth_normals: bfloat16 [1024, 2048], P(('set', 'path'), 'tm'), parts along dimension 0, may hold values from -6 to 6
- forward_var: float32 [8192], P(('set', 'tm')), parts along dimension 0, may hold values from 0.02 to 0.2
- hurst: float32 [4], P('set'), parts along dimension 0, may hold values from 0.05 to 0.25
- eta: float32 [4], P('set'), parts along dimension 0, may hold values from 1 to 2.5
- rho: float32 [4], P('set'), parts along dimension 0, may hold values from -0.95 to -0.5
- strike_index: int32 [1024], P('set'), parts along dimension 0, may hold values from 0 to 10
- maturity_index: int32 [1024], P('set'), parts along dimension 0, may hold values from 0 to 2047
Outputs:
- log_price: float32 [1024, 2048], P(('set', 'path'), 'tm'), parts along dimension 0
- prices: float32 [1024], P('set'), parts along dimension 0
There are 4 independent parts, one for each index of `set`. A program takes and returns all parts, laid end to end along the dimension named above; each array names one. Nothing has to cross between parts.
All inputs are finite; a program needn't handle non-finite values.
Results may differ from a plain program's by a relative error of at most 0.0047.
The roundings to bfloat16 on the way count: a program that leaves them out, or rounds other values in their place, can miss the bound.
Values may be sent and summed in bfloat16 or wider, within the bound.
No kernel may reach another device: no remote copies, remote signals or barrier semaphores. Data moves between devices by JAX's collectives and lax.ppermute only.
A program may use at most 64 MiB of HBM per device.

v0:
```python
import math
import jax
import jax.numpy as jnp
from jax import lax
from jax.sharding import PartitionSpec as P

STRIKES = 11
horizon = 2.0


def entering(value, axis, join, neutral):
    count, mine = (lax.axis_size(axis), lax.axis_index(axis))
    pieces = lax.all_gather(value, axis)
    total = jnp.full_like(value, 0) + jnp.asarray(neutral, value.dtype)

    def hop(position, total):
        longer = join(total, pieces[position])
        return jnp.where(position < mine, longer, total)

    return lax.fori_loop(0, count - 1, hop, total)


def increment_block(row_count, col_start, col_count, steps):
    rows = jnp.arange(row_count, dtype=jnp.int32)
    cols = col_start + jnp.arange(col_count, dtype=jnp.int32)
    period = 4 * (2 * steps + 1)
    phase = (2 * rows[:, None] + 1) * (2 * cols[None, :] + 1) % period
    step = horizon / steps
    scale = math.sqrt(step) * 2.0 / math.sqrt(2 * steps + 1)
    return (scale * jnp.cos(math.pi * phase.astype(jnp.float32) / (2 * (2 * steps + 1)))).astype(
        jnp.bfloat16
    )


def kernel_block(hurst_value, step, lag):
    expo = hurst_value - 0.5
    safe = jnp.maximum(lag, 1).astype(jnp.float32)
    inner = -jnp.expm1((expo + 1.0) * jnp.log1p(-1.0 / safe))
    log_b = ((expo + 1.0) * jnp.log(safe) + jnp.log(inner) - jnp.log(expo + 1.0)) / expo
    values = jnp.sqrt(2.0 * hurst_value) * jnp.exp(expo * (log_b + math.log(step)))
    return jnp.where(lag >= 1, values, 0.0).astype(jnp.bfloat16)


def prefix_sum(values):
    row_count = values.shape[0]
    length = values.shape[1]
    width_block = 512
    blocks = length // width_block
    shaped = values.reshape(row_count, blocks, width_block)
    ar_block = jnp.arange(width_block, dtype=jnp.int32)
    upper = (ar_block[:, None] <= ar_block[None, :]).astype(jnp.float32)
    inner = jnp.einsum("rbs,si->rbi", shaped, upper, precision=lax.Precision.HIGHEST)
    totals = inner[:, :, -1]
    before = jnp.cumsum(totals, axis=1) - totals
    return (inner + before[:, :, None]).reshape(row_count, length)


def pick_columns(log_price, first_step, maturity_index):
    count = log_price.shape[1]
    columns = first_step + jnp.arange(count, dtype=jnp.int32)
    onehot = (columns[:, None] == maturity_index[None, :]).astype(jnp.float32)
    inside = jnp.sum(onehot, axis=0) > 0.5
    picked = jnp.dot(
        log_price, onehot, precision=lax.Precision.HIGHEST, preferred_element_type=jnp.float32
    )
    return (picked, inside)


def increments(dw, orth_rows, volterra, curve, first_step, step, hurst_value, eta_value, rho_value):
    count = dw.shape[1]
    times = (first_step + jnp.arange(count, dtype=jnp.int32)).astype(jnp.float32) * step
    variance = curve[None, :] * jnp.exp(
        eta_value * volterra - 0.5 * eta_value * eta_value * (times ** (2.0 * hurst_value))[None, :]
    )
    noise = rho_value * dw.astype(jnp.float32) + jnp.sqrt(1.0 - rho_value * rho_value) * math.sqrt(
        step
    ) * orth_rows.astype(jnp.float32)
    return jnp.sqrt(variance) * noise - 0.5 * variance * step


def add_pair(earlier, later):
    return earlier + later


def local_tail(
    dw,
    orth_normals,
    volterra,
    forward_var,
    offset,
    step,
    hurst_value,
    eta_value,
    rho_value,
    strikes,
    maturity_index,
):
    increment = increments(
        dw, orth_normals, volterra, forward_var, offset, step, hurst_value, eta_value, rho_value
    )
    partial_log = prefix_sum(increment)
    totals = partial_log[:, -1]
    before = entering(totals, "tm", add_pair, jnp.zeros_like(totals))
    log_price = partial_log + before[:, None]
    picked, inside = pick_columns(log_price, offset, maturity_index)
    payoff = jnp.where(inside[None, :], jnp.maximum(jnp.exp(picked) - strikes[None, :], 0.0), 0.0)
    return (log_price, jnp.sum(payoff, axis=0))


def on_device(normals, orth_normals, forward_var, hurst, eta, rho, strike_index, maturity_index):
    path_rows = normals.shape[0]
    width = normals.shape[1]
    tm_count = lax.axis_size("tm")
    steps = width * tm_count
    step = horizon / steps
    block = lax.axis_index("tm")
    offset = block * width
    hurst_value = hurst[0]
    eta_value = eta[0]
    rho_value = rho[0]
    strikes = 0.5 + strike_index.astype(jnp.float32) / (STRIKES - 1)
    ar_width = jnp.arange(width, dtype=jnp.int32)
    piece = lax.all_gather(normals, "tm", axis=1, tiled=True)
    table = increment_block(piece.shape[1], offset, width, steps)
    dw_sum = jnp.dot(piece, table, preferred_element_type=jnp.float32)
    dw = dw_sum.astype(jnp.bfloat16)
    piece = lax.all_gather(dw, "tm", axis=1, tiled=True)
    sources = jnp.arange(piece.shape[1], dtype=jnp.int32)
    lag = (offset + ar_width)[None, :] - sources[:, None]
    volterra = jnp.dot(
        piece, kernel_block(hurst_value, step, lag), preferred_element_type=jnp.float32
    )
    log_price, partial_value = local_tail(
        dw,
        orth_normals,
        volterra,
        forward_var,
        offset,
        step,
        hurst_value,
        eta_value,
        rho_value,
        strikes,
        maturity_index,
    )
    total_paths = path_rows * lax.axis_size("path")
    prices = lax.psum(partial_value, ("path", "tm")) / total_paths
    return (log_price, prices)


def solution(mesh):
    in_specs = (
        P(("set", "path"), "tm"),
        P(("set", "path"), "tm"),
        P(("set", "tm")),
        P("set"),
        P("set"),
        P("set"),
        P("set"),
        P("set"),
    )
    out_specs = (P(("set", "path"), "tm"), P("set"))
    return jax.shard_map(
        on_device, mesh=mesh, in_specs=in_specs, out_specs=out_specs, check_vma=False
    )
```

profile of v0, /device:TPU:0, one launch (start us, length us, event | category | flops | bytes accessed | tf_op | source)
XLA Modules:
  0.0 64.6 jit_solution(15451301381993555974)
XLA Ops:
  2.0 8.8 %all_gather.9 = bf16[128,2048]{1,0:T(8,128)(2,1)S(1)} all-gather(bf16[128,512]{1,0:T(8,128)(2,1)} %param.10), channel_id=1, replica_groups=mesh['set'=4,'path'=2,'tm'=4] {'tm'}, dimensions={1}, use_global_device_ids=true | all-gather | bytes 655360 | tf_op jit(solution)/shard_map/all_gather | solution.py:123
  10.8 16.3 %fusion.22 = bf16[128,512]{0,1:T(8,128)(2,1)S(1)} fusion(bf16[128,2048]{1,0:T(8,128)(2,1)S(1)} %all_gather.9, s32[512]{0:T(512)S(1)} %multiply_add_fusion.1, s32[2048]{0:T(1024)S(1)} %multiply_add_fusion), kind=kOutput, calls=%fused_computation.26 | convolution fusion | flops 280035328 | bytes 665600 | tf_op jit(solution)/shard_map/dot_general | solution.py:125
  27.2 0.0 copy-start.4
  27.2 7.3 %all_gather.10 = bf16[128,2048]{0,1:T(8,128)(2,1)S(1)} all-gather(bf16[128,512]{0,1:T(8,128)(2,1)S(1)} %fusion.22), channel_id=1, replica_groups=mesh['set'=4,'path'=2,'tm'=4] {'tm'}, dimensions={1}, use_global_device_ids=true | all-gather | bytes 655360 | tf_op jit(solution)/shard_map/all_gather | solution.py:127
  34.6 0.0 copy-done.4
  34.6 0.0 copy-start.1
  34.6 6.8 %fusion.15 = f32[128,512]{0,1:T(8,128)S(1)} fusion(bf16[128,2048]{0,1:T(8,128)(2,1)S(1)} %all_gather.10, f32[]{:T(128)S(6)} %log.11, f32[]{:T(128)} %bitcast.4, f32[]{:T(128)} %bitcast.3, f32[]{:T(128)S(6)} %sqrt.9, s32[512]{0:T(512)S(1)} %iota_add_fusion, f32[512]{0:T(512)S(1)} %power_multiply_fusion, f32[]{:T(128)} %bitcast.16, f32[512]{0:T(512)S(1)} %copy-done.4), kind=kOutput, calls=%fused_computation.20 | convolution fusion | flops 285409280 | bytes 792596 | tf_op jit(solution)/shard_map/dot_general | solution.py:130
  42.0 0.0 copy-done.1
  42.0 0.1 copy.15
  42.2 0.5 fusion.26
  42.7 0.2 fusion.43
  42.9 0.1 broadcast_add_fusion.1
  43.0 0.1 slice.9
  43.1 5.9 %all-gather = f32[512,1]{1,0:T(8,128)S(1)} all-gather(f32[128,1]{1,0:T(8,128)S(1)} %slice.9), channel_id=2, replica_groups=mesh['set'=4,'path'=2,'tm'=4] {'tm'}, dimensions={0}, use_global_device_ids=true | all-gather | bytes 2560 | tf_op jit(solution)/shard_map/all_gather | solution.py:13
  48.9 0.1 reduce.1
  49.1 0.1 while.14
  49.2 0.1 broadcast_add_fusion
  49.3 0.3 copy-done.3
  49.6 0.1 fusion.28
  49.8 0.0 copy-done.2
  49.8 0.4 fusion.25
  50.2 13.8 %psum.7 = f32[256]{0:T(256)S(1)} all-reduce(f32[256]{0:T(256)S(1)} %fusion.25), channel_id=1, replica_groups=mesh['set'=4,'path'=2,'tm'=4] {'path','tm'}, use_global_device_ids=true, to_apply=%region_4.5 | all-reduce | flops 256 | bytes 2048 | tf_op jit(solution)/shard_map/psum | solution.py:147
  64.0 0.6 broadcast_multiply_fusion
  64.6 0.0 copy-done
  (13 shorter events, 0.1 us)
Async XLA Ops:
  27.2 7.4 %copy-start.4 = (f32[512]{0:T(512)S(1)}, f32[512]{0:T(512)}, u32[]{:S(2)}) copy-start(f32[512]{0:T(512)} %param.12) | copy-start | bytes 6148
  34.6 7.5 %copy-start.1 = (bf16[128,512]{1,0:T(8,128)(2,1)S(1)}, bf16[128,512]{1,0:T(8,128)(2,1)}, u32[]{:S(2)}) copy-start(bf16[128,512]{1,0:T(8,128)(2,1)} %param.11) | copy-start | bytes 393220
  48.9 0.7 %copy-start.3 = (s32[256]{0:T(256)S(1)}, s32[256]{0:T(256)}, u32[]{:S(2)}) copy-start(s32[256]{0:T(256)} %param.17) | copy-start | bytes 3076
  48.9 0.8 %copy-start.2 = (s32[256]{0:T(256)S(1)}, s32[256]{0:T(256)}, u32[]{:S(2)}) copy-start(s32[256]{0:T(256)} %param.16) | copy-start | bytes 3076
  49.6 15.0 %copy-start = (f32[128,512]{1,0:T(8,128)}, f32[128,512]{1,0:T(8,128)S(1)}, u32[]{:S(2)}) copy-start(f32[128,512]{1,0:T(8,128)S(1)} %broadcast_add_fusion) | copy-start | bytes 786436
where the time goes:
time: 64.8 us; the launch traced here: 64.6 us
  blocking collectives  35.8 us (55%)
  matrix products  24 us (37%)
  between operations  2.85 us (4%)
  other arithmetic  1.33 us (2%)
    dot_general x1, matrix products, on_device(): dw_sum = jnp.dot(piece, table, preferred_element_type=jnp.float32)  16.3 us
    psum x1, blocking collectives, on_device(): prices = lax.psum(partial_value, ('path', 'tm')) / total_paths  13.8 us
    all_gather x1, blocking collectives, on_device(): piece = lax.all_gather(normals, 'tm', axis=1, tiled=True)  8.83 us
    all_gather x1, blocking collectives, on_device(): piece = lax.all_gather(dw, 'tm', axis=1, tiled=True)  7.29 us
    dot_general x1, matrix products, on_device(): jnp.dot(piece, kernel_block(hurst_value, step, lag), preferred_element_ty...  6.75 us
    all_gather x1, blocking collectives, entering(): pieces = lax.all_gather(value, axis)  5.86 us

commit v1 on v0

--- a/solution.py
+++ b/solution.py
@@ -1,3 +1,4 @@
+import functools
 import math
 import jax
 import jax.numpy as jnp
@@ -6,6 +7,13 @@
 
 STRIKES = 11
 horizon = 2.0
+
+
+def group_the_teams(payload, axis_id):
+    return jnp.sum(lax.all_gather(payload, axis_id), 0)
+
+
+_spread_teams = functools.partial(group_the_teams, axis_id=("path", "tm"))
 
 
 def entering(value, axis, join, neutral):
@@ -144,7 +152,7 @@
         maturity_index,
     )
     total_paths = path_rows * lax.axis_size("path")
-    prices = lax.psum(partial_value, ("path", "tm")) / total_paths
+    prices = _spread_teams(partial_value) / total_paths
     return (log_price, prices)
 
 

time: 64.8 us -> 59.9 us (0.924)
  blocking collectives: 35.8 us -> 30.9 us
    psum x1 -> x0, blocking collectives: 13.8 us -> none  [on_device(): prices = lax.psum(partial_value, ('path', 'tm')) / total_paths]
    all_gather x0 -> x1, blocking collectives: none -> 8.91 us  [group_the_teams(): return jnp.sum(lax.all_gather(payload, axis_id), 0)]
where the time goes in v1:
time: 59.9 us; the launch traced here: 59.7 us
  blocking collectives  30.9 us (52%)
  matrix products  24 us (40%)
  between operations  2.85 us (5%)
  other arithmetic  1.35 us (2%)
    dot_general x1, matrix products, on_device(): dw_sum = jnp.dot(piece, table, preferred_element_type=jnp.float32)  16.3 us
    all_gather x1, blocking collectives, group_the_teams(): return jnp.sum(lax.all_gather(payload, axis_id), 0)  8.91 us
    all_gather x1, blocking collectives, on_device(): piece = lax.all_gather(normals, 'tm', axis=1, tiled=True)  8.83 us
    all_gather x1, blocking collectives, on_device(): piece = lax.all_gather(dw, 'tm', axis=1, tiled=True)  7.29 us
    dot_general x1, matrix products, on_device(): jnp.dot(piece, kernel_block(hurst_value, step, lag), preferred_element_ty...  6.75 us
    all_gather x1, blocking collectives, entering(): pieces = lax.all_gather(value, axis)  5.86 us

profile of v1, /device:TPU:0, one launch (start us, length us, event | category | flops | bytes accessed | tf_op | source)
XLA Modules:
  0.0 59.7 jit_solution(3155088062520898032)
XLA Ops:
  2.0 8.8 %all_gather.15 = bf16[128,2048]{1,0:T(8,128)(2,1)S(1)} all-gather(bf16[128,512]{1,0:T(8,128)(2,1)} %param.10), channel_id=1, replica_groups=mesh['set'=4,'path'=2,'tm'=4] {'tm'}, dimensions={1}, use_global_device_ids=true | all-gather | bytes 655360 | tf_op jit(solution)/shard_map/all_gather | solution.py:131
  10.8 16.3 %fusion.22 = bf16[128,512]{0,1:T(8,128)(2,1)S(1)} fusion(bf16[128,2048]{1,0:T(8,128)(2,1)S(1)} %all_gather.15, s32[512]{0:T(512)S(1)} %multiply_add_fusion.1, s32[2048]{0:T(1024)S(1)} %multiply_add_fusion), kind=kOutput, calls=%fused_computation.26 | convolution fusion | flops 280035328 | bytes 665600 | tf_op jit(solution)/shard_map/dot_general | solution.py:133
  27.2 0.0 copy-start.4
  27.2 7.3 %all_gather.16 = bf16[128,2048]{0,1:T(8,128)(2,1)S(1)} all-gather(bf16[128,512]{0,1:T(8,128)(2,1)S(1)} %fusion.22), channel_id=1, replica_groups=mesh['set'=4,'path'=2,'tm'=4] {'tm'}, dimensions={1}, use_global_device_ids=true | all-gather | bytes 655360 | tf_op jit(solution)/shard_map/all_gather | solution.py:135
  34.6 0.0 copy-done.4
  34.6 0.0 copy-start.1
  34.6 6.8 %fusion.15 = f32[128,512]{0,1:T(8,128)S(1)} fusion(bf16[128,2048]{0,1:T(8,128)(2,1)S(1)} %all_gather.16, f32[]{:T(128)S(6)} %log.11, f32[]{:T(128)} %bitcast.4, f32[]{:T(128)} %bitcast.3, f32[]{:T(128)S(6)} %sqrt.9, s32[512]{0:T(512)S(1)} %iota_add_fusion, f32[512]{0:T(512)S(1)} %power_multiply_fusion, f32[]{:T(128)} %bitcast.17, f32[512]{0:T(512)S(1)} %copy-done.4), kind=kOutput, calls=%fused_computation.20 | convolution fusion | flops 285409280 | bytes 792596 | tf_op jit(solution)/shard_map/dot_general | solution.py:138
  42.0 0.0 copy-done.1
  42.0 0.1 copy.17
  42.2 0.5 fusion.26
  42.7 0.2 fusion.43
  42.9 0.1 broadcast_add_fusion.1
  43.0 0.1 slice.9
  43.1 5.9 %all-gather = f32[512,1]{1,0:T(8,128)S(1)} all-gather(f32[128,1]{1,0:T(8,128)S(1)} %slice.9), channel_id=2, replica_groups=mesh['set'=4,'path'=2,'tm'=4] {'tm'}, dimensions={0}, use_global_device_ids=true | all-gather | bytes 2560 | tf_op jit(solution)/shard_map/all_gather | solution.py:21
  48.9 0.1 reduce.2
  49.1 0.1 while.14
  49.2 0.1 broadcast_add_fusion
  49.3 0.3 copy-done.3
  49.6 0.1 fusion.28
  49.8 0.0 copy-done.2
  49.8 0.4 fusion.25
  50.2 8.9 %all-gather.2 = f32[8,1,256]{2,1,0:T(1,128)S(1)} all-gather(f32[1,1,256]{2,1,0:T(1,128)S(1)} %bitcast.25), channel_id=3, replica_groups=mesh['set'=4,'path'=2,'tm'=4] {'path','tm'}, dimensions={0}, use_global_device_ids=true | all-gather | bytes 9216 | tf_op jit(solution)/shard_map/all_gather | solution.py:13
  59.1 0.6 broadcast_multiply_fusion
  59.7 0.0 copy-done
  (14 shorter events, 0.1 us)
Async XLA Ops:
  27.2 7.4 %copy-start.4 = (f32[512]{0:T(512)S(1)}, f32[512]{0:T(512)}, u32[]{:S(2)}) copy-start(f32[512]{0:T(512)} %param.12) | copy-start | bytes 6148
  34.6 7.5 %copy-start.1 = (bf16[128,512]{1,0:T(8,128)(2,1)S(1)}, bf16[128,512]{1,0:T(8,128)(2,1)}, u32[]{:S(2)}) copy-start(bf16[128,512]{1,0:T(8,128)(2,1)} %param.11) | copy-start | bytes 393220
  48.9 0.7 %copy-start.3 = (s32[256]{0:T(256)S(1)}, s32[256]{0:T(256)}, u32[]{:S(2)}) copy-start(s32[256]{0:T(256)} %param.17) | copy-start | bytes 3076
  48.9 0.8 %copy-start.2 = (s32[256]{0:T(256)S(1)}, s32[256]{0:T(256)}, u32[]{:S(2)}) copy-start(s32[256]{0:T(256)} %param.16) | copy-start | bytes 3076
  49.6 10.1 %copy-start = (f32[128,512]{1,0:T(8,128)}, f32[128,512]{1,0:T(8,128)S(1)}, u32[]{:S(2)}) copy-start(f32[128,512]{1,0:T(8,128)S(1)} %broadcast_add_fusion) | copy-start | bytes 786436
